TPU v7x, 512 devices: a whole 4x4x16 slice. The times are simulated.
512 devices in a mesh: seq: 32 (over z, core), head: 16 (over y, x).
Axes of the slice: x: 4, y: 4, z: 16, core: 2. Of those that a mesh axis runs over, the one named last changes fastest.
Arguments:
- hidden_in: bfloat16 [8192, 4096], P('seq'), may hold values from -6 to 6
- w_qkv: bfloat16 [3, 4096, 4096], P(None, 'seq', 'head'), may hold values from -0.09375 to 0.09375
- doc_starts: int32 [9], replicated, may hold values from 0 to 8191, as said below
- beta_codes: int32 [8192, 32], P('seq', 'head'), may hold values from 0 to 4, as said below
- w_out: bfloat16 [4096, 4096], P('head', 'seq'), may hold values from -0.1875 to 0.1875
Outputs:
- layer_out: bfloat16 [8192, 4096], P('seq', 'head')
Inputs may be any that keep to these rules, and one draw needn't show every extreme that they name: `doc_starts`: strictly rising; the first is 0 and the last is 8191, a one-token final document. `beta_codes`: integer codes of the write strength beta = 1.6 + 0.1 * code.
All inputs are finite; a program needn't handle non-finite values.
Results may differ from a plain program's by a relative error of at most 0.02.
Values may be sent and summed in bfloat16 or wider, within the bound.
No kernel may reach another device: no remote copies, remote signals or barrier semaphores. Data moves between devices by JAX's collectives and lax.ppermute only.
A program may use at most 64 MiB of HBM per device.

v0:
```python
import jax
import jax.numpy as jnp
from jax import lax
from jax.sharding import PartitionSpec as P

highest_accuracy = lax.Precision.HIGHEST


def passed_along(value, axis, steps):
    count = lax.axis_size(axis)
    first, last = (max(0, -steps), min(count, count - steps))
    return lax.ppermute(value, axis, [(source, source + steps) for source in range(first, last)])


def bmatmul(left, right):
    return jnp.einsum("hij,hjk->hik", left, right, precision=highest_accuracy)


def unit_rows(matrix):
    return matrix * lax.rsqrt(jnp.sum(matrix * matrix, axis=-1, keepdims=True) + 1e-06)


def block_terms(query_blk, key_blk, value_blk, beta_blk, doc_blk):
    block_len = query_blk.shape[1]
    head_size = query_blk.shape[2]
    row_ids = lax.broadcasted_iota(jnp.int32, (block_len, block_len), 0)
    col_ids = lax.broadcasted_iota(jnp.int32, (block_len, block_len), 1)
    same_document = doc_blk[:, None] == doc_blk[None, :]
    strict_mask = same_document & (col_ids < row_ids)
    incl_mask = same_document & (col_ids <= row_ids)
    carry_in = (doc_blk == 0).astype(jnp.float32)
    last_doc = (doc_blk == doc_blk[-1]).astype(jnp.float32)
    last_keep = carry_in[-1]
    key_gram = jnp.einsum("hts,hus->htu", key_blk, key_blk, precision=highest_accuracy)
    system = jnp.eye(block_len, dtype=jnp.float32)[None] + jnp.where(
        strict_mask[None], beta_blk[:, :, None] * key_gram, 0.0
    )
    right_side = beta_blk[:, :, None] * jnp.concatenate(
        [value_blk, carry_in[None, :, None] * key_blk], axis=-1
    )
    solved = jax.scipy.linalg.solve_triangular(system, right_side, lower=True, unit_diagonal=True)
    fresh_vals = solved[..., :head_size]
    mixed_keys = solved[..., head_size:]
    query_key = jnp.where(
        incl_mask[None],
        jnp.einsum("hts,hus->htu", query_blk, key_blk, precision=highest_accuracy),
        0.0,
    )
    local_out = bmatmul(query_key, fresh_vals)
    carry_map = carry_in[None, :, None] * query_blk - bmatmul(query_key, mixed_keys)
    tail_keys = last_doc[None, :, None] * key_blk
    trans_map = last_keep * jnp.eye(head_size, dtype=jnp.float32)[None] - jnp.einsum(
        "hts,htu->hsu", tail_keys, mixed_keys, precision=highest_accuracy
    )
    state_add = jnp.einsum("hts,htv->hsv", tail_keys, fresh_vals, precision=highest_accuracy)
    return (carry_map, local_out, trans_map, state_add)


def per_device(hidden_in, w_qkv, doc_starts, beta_codes, w_out):
    tok_rows = hidden_in.shape[0]
    head_count = beta_codes.shape[1]
    feat_width = w_qkv.shape[2]
    head_size = feat_width // head_count
    projected = jnp.einsum(
        "td,pde->pte",
        hidden_in,
        lax.all_gather(w_qkv, "seq", axis=1, tiled=True),
        preferred_element_type=jnp.float32,
    ).astype(jnp.bfloat16)
    block_len = min(128, tok_rows)
    block_count = tok_rows // block_len

    def to_blocks(matrix):
        shaped = matrix.astype(jnp.float32).reshape(block_count, block_len, head_count, head_size)
        return jnp.transpose(shaped, (0, 2, 1, 3))

    queries = to_blocks(
        unit_rows(projected[0].astype(jnp.float32).reshape(tok_rows, head_count, head_size))
    )
    keys_all = to_blocks(
        unit_rows(projected[1].astype(jnp.float32).reshape(tok_rows, head_count, head_size))
    )
    values_all = to_blocks(projected[2])
    betas = 1.6 + 0.1 * beta_codes.astype(jnp.float32)
    betas = jnp.transpose(betas.reshape(block_count, block_len, head_count), (0, 2, 1))
    positions = lax.axis_index("seq") * tok_rows + jnp.arange(tok_rows, dtype=jnp.int32)
    is_start = jnp.any(positions[:, None] == doc_starts[None, :], axis=1).astype(jnp.int32)
    doc_index = jnp.cumsum(is_start.reshape(block_count, block_len), axis=1)
    blocks = (queries, keys_all, values_all, betas, doc_index)
    identity_mat = jnp.broadcast_to(
        jnp.eye(head_size, dtype=jnp.float32), (head_count, head_size, head_size)
    )
    zero_state = jnp.zeros((head_count, head_size, head_size), jnp.float32)

    def local_step(carry, block_in):
        transit, local_state = carry
        carry_map, local_out, trans_map, state_add = block_terms(*block_in)
        partial_out = local_out + bmatmul(carry_map, local_state)
        correction = bmatmul(carry_map, transit)
        return (
            (bmatmul(trans_map, transit), bmatmul(trans_map, local_state) + state_add),
            (partial_out, correction),
        )

    (transit, local_state), (partial_out, correction) = lax.scan(
        local_step, (identity_mat, zero_state), blocks
    )

    def relay(turn_index, incoming):
        return passed_along(
            (bmatmul(transit, incoming) + local_state).astype(jnp.bfloat16), "seq", 1
        ).astype(jnp.float32)

    state_in = lax.fori_loop(0, lax.axis_size("seq") - 1, relay, zero_state)

    def rerun_step(state_now, block_in):
        carry_map, local_out, trans_map, state_add = block_terms(*block_in)
        result = local_out + bmatmul(carry_map, state_now)
        return (bmatmul(trans_map, state_now) + state_add, result)

    final_state, outputs = lax.scan(rerun_step, state_in, blocks)
    outputs = jnp.transpose(outputs, (0, 2, 1, 3)).reshape(tok_rows, head_count, head_size)
    normed = outputs * lax.rsqrt(jnp.mean(outputs * outputs, axis=-1, keepdims=True) + 1e-05)
    normed = normed.astype(jnp.bfloat16).reshape(tok_rows, feat_width)
    terms = jnp.dot(
        normed, lax.all_gather(w_out, "seq", axis=1, tiled=True), preferred_element_type=jnp.float32
    )
    return lax.psum_scatter(terms.astype(jnp.bfloat16), "head", scatter_dimension=1, tiled=True)


def solution(mesh):
    in_specs = (P("seq", None), P(None, "seq", "head"), P(), P("seq", "head"), P("head", "seq"))
    out_specs = P("seq", "head")
    return jax.shard_map(
        per_device, mesh=mesh, in_specs=in_specs, out_specs=out_specs, check_vma=False
    )
```

profile of v0, /device:TPU:2, one launch (start us, length us, event | category | flops | bytes accessed | tf_op | source)
XLA Modules:
  0.0 534.2 jit_solution(8153678685199269172)
XLA Ops:
  11.1 91.4 %all-gather.3.cloned.1.call-done = bf16[3,4096,256]{1,2,0:T(8,128)(2,1)} async-done(((bf16[3,128,256]{1,2,0:T(8,128)(2,1)}), bf16[3,4096,256]{1,2,0:T(8,128)(2,1)}) %all-gather.3.cloned.1.call-update) | async-done | bytes 6291472 | tf_op jit(solution)/shard_map/all_gather | solution.py:67
  114.2 49.7 %while.37 = (s32[]{:T(128)}, f32[2,128,128]{2,1,0:T(8,128)S(1)}, f32[2,128,128]{2,1,0:T(8,128)S(1)}, s32[2,128]{1,0:T(2,128)S(1)}, f32[2,2,128,128]{3,2,1,0:T(8,...) while((s32[]{:T(128)}, f32[2,128,128]{2,1,0:T(8,128)S(1)}, ...), condition=%wide.region_4.6_spmd.clone, body=%wide.region_3.5_spmd.clone.sunk | while | flops 352977536 | bytes 3876507 | solution.py:105
  115.0 19.7 %custom-call.12 = f32[2,1,128,128]{2,3,1,0:T(8,128)S(1)} custom-call(f32[2,1,128,128]{3,2,1,0:T(8,128)S(1)} %fusion.169), custom_call_target="InvertDiagBlocksLowerTriangular" | custom-call | tf_op jit(solution)/shard_map/while/body/eval_jaxpr/jit(_solve_triangular)/vmap()/triangular_solve | solution.py:41
  139.7 19.7 %custom-call.12 = f32[2,1,128,128]{2,3,1,0:T(8,128)S(1)} custom-call(f32[2,1,128,128]{3,2,1,0:T(8,128)S(1)} %fusion.169), custom_call_target="InvertDiagBlocksLowerTriangular" | custom-call | tf_op jit(solution)/shard_map/while/body/eval_jaxpr/jit(_solve_triangular)/vmap()/triangular_solve | solution.py:41
  163.8 194.0 %while.38 = (s32[]{:T(128)}, f32[2,128,128]{2,1,0:T(8,128)S(1)}, f32[2,128,128]{2,1,0:T(8,128)S(1)}, f32[2,128,128]{2,1,0:T(8,128)S(1)}, s32[]{:T(128)}, /*index=5*/s32[]{:T(128)}) while((s32[]{:T(128)}, f32[2,128,128]{2,1,0:T(8,128)S(1)}, f32[2,128,128]{2,1,0:T(8,128)S(1)}, f32[2,128,128]{2,1,0:T(8,128)S(1)}, s32[]{:T(128)}, ...), condition=%wide.region_6.8_spmd.clone, body=%wide.region_5.7_spmd.clone.sunk | while | flops 50462720 | bytes 917623 | solution.py:114
  177.2 4.7 collective-permute-start
  183.1 4.7 collective-permute-start
  189.0 4.7 collective-permute-start
  194.9 4.7 collective-permute-start
  200.8 4.7 collective-permute-start
  206.7 4.7 collective-permute-start
  212.6 4.7 collective-permute-start
  218.5 4.7 collective-permute-start
  224.4 4.7 collective-permute-start
  259.7 4.8 collective-permute-start
  265.7 5.9 %collective-permute-start = (bf16[2,128,128]{2,1,0:T(8,128)(2,1)S(1)}, bf16[2,128,128]{2,1,0:T(8,128)(2,1)S(1)}, u32[]{:S(2)}, u32[]{:S(2)}) collective-permute-start(bf16[2,128,128]{2,1,0:T(8,128)(2,1)S(1)} %fusion.176), channel_id=1, source_target_pairs={{0,16},{16,32},{32,48},{48,64},{64,80},{80,96},{96,112},{112,128},... | collective-permute-start | bytes 196616 | tf_op jit(solution)/shard_map/while/body/eval_jaxpr/ppermute | solution.py:12
  272.8 5.9 %collective-permute-start = (bf16[2,128,128]{2,1,0:T(8,128)(2,1)S(1)}, bf16[2,128,128]{2,1,0:T(8,128)(2,1)S(1)}, u32[]{:S(2)}, u32[]{:S(2)}) collective-permute-start(bf16[2,128,128]{2,1,0:T(8,128)(2,1)S(1)} %fusion.176), channel_id=1, source_target_pairs={{0,16},{16,32},{32,48},{48,64},{64,80},{80,96},{96,112},{112,128},... | collective-permute-start | bytes 196616 | tf_op jit(solution)/shard_map/while/body/eval_jaxpr/ppermute | solution.py:12
  279.9 5.9 %collective-permute-start = (bf16[2,128,128]{2,1,0:T(8,128)(2,1)S(1)}, bf16[2,128,128]{2,1,0:T(8,128)(2,1)S(1)}, u32[]{:S(2)}, u32[]{:S(2)}) collective-permute-start(bf16[2,128,128]{2,1,0:T(8,128)(2,1)S(1)} %fusion.176), channel_id=1, source_target_pairs={{0,16},{16,32},{32,48},{48,64},{64,80},{80,96},{96,112},{112,128},... | collective-permute-start | bytes 196616 | tf_op jit(solution)/shard_map/while/body/eval_jaxpr/ppermute | solution.py:12
  287.0 5.9 %collective-permute-start = (bf16[2,128,128]{2,1,0:T(8,128)(2,1)S(1)}, bf16[2,128,128]{2,1,0:T(8,128)(2,1)S(1)}, u32[]{:S(2)}, u32[]{:S(2)}) collective-permute-start(bf16[2,128,128]{2,1,0:T(8,128)(2,1)S(1)} %fusion.176), channel_id=1, source_target_pairs={{0,16},{16,32},{32,48},{48,64},{64,80},{80,96},{96,112},{112,128},... | collective-permute-start | bytes 196616 | tf_op jit(solution)/shard_map/while/body/eval_jaxpr/ppermute | solution.py:12
  294.2 5.9 %collective-permute-start = (bf16[2,128,128]{2,1,0:T(8,128)(2,1)S(1)}, bf16[2,128,128]{2,1,0:T(8,128)(2,1)S(1)}, u32[]{:S(2)}, u32[]{:S(2)}) collective-permute-start(bf16[2,128,128]{2,1,0:T(8,128)(2,1)S(1)} %fusion.176), channel_id=1, source_target_pairs={{0,16},{16,32},{32,48},{48,64},{64,80},{80,96},{96,112},{112,128},... | collective-permute-start | bytes 196616 | tf_op jit(solution)/shard_map/while/body/eval_jaxpr/ppermute | solution.py:12
  301.3 5.9 %collective-permute-start = (bf16[2,128,128]{2,1,0:T(8,128)(2,1)S(1)}, bf16[2,128,128]{2,1,0:T(8,128)(2,1)S(1)}, u32[]{:S(2)}, u32[]{:S(2)}) collective-permute-start(bf16[2,128,128]{2,1,0:T(8,128)(2,1)S(1)} %fusion.176), channel_id=1, source_target_pairs={{0,16},{16,32},{32,48},{48,64},{64,80},{80,96},{96,112},{112,128},... | collective-permute-start | bytes 196616 | tf_op jit(solution)/shard_map/while/body/eval_jaxpr/ppermute | solution.py:12
  308.4 5.9 %collective-permute-start = (bf16[2,128,128]{2,1,0:T(8,128)(2,1)S(1)}, bf16[2,128,128]{2,1,0:T(8,128)(2,1)S(1)}, u32[]{:S(2)}, u32[]{:S(2)}) collective-permute-start(bf16[2,128,128]{2,1,0:T(8,128)(2,1)S(1)} %fusion.176), channel_id=1, source_target_pairs={{0,16},{16,32},{32,48},{48,64},{64,80},{80,96},{96,112},{112,128},... | collective-permute-start | bytes 196616 | tf_op jit(solution)/shard_map/while/body/eval_jaxpr/ppermute | solution.py:12
  315.5 5.9 %collective-permute-start = (bf16[2,128,128]{2,1,0:T(8,128)(2,1)S(1)}, bf16[2,128,128]{2,1,0:T(8,128)(2,1)S(1)}, u32[]{:S(2)}, u32[]{:S(2)}) collective-permute-start(bf16[2,128,128]{2,1,0:T(8,128)(2,1)S(1)} %fusion.176), channel_id=1, source_target_pairs={{0,16},{16,32},{32,48},{48,64},{64,80},{80,96},{96,112},{112,128},... | collective-permute-start | bytes 196616 | tf_op jit(solution)/shard_map/while/body/eval_jaxpr/ppermute | solution.py:12
  322.6 5.9 %collective-permute-start = (bf16[2,128,128]{2,1,0:T(8,128)(2,1)S(1)}, bf16[2,128,128]{2,1,0:T(8,128)(2,1)S(1)}, u32[]{:S(2)}, u32[]{:S(2)}) collective-permute-start(bf16[2,128,128]{2,1,0:T(8,128)(2,1)S(1)} %fusion.176), channel_id=1, source_target_pairs={{0,16},{16,32},{32,48},{48,64},{64,80},{80,96},{96,112},{112,128},... | collective-permute-start | bytes 196616 | tf_op jit(solution)/shard_map/while/body/eval_jaxpr/ppermute | solution.py:12
  329.7 5.9 %collective-permute-start = (bf16[2,128,128]{2,1,0:T(8,128)(2,1)S(1)}, bf16[2,128,128]{2,1,0:T(8,128)(2,1)S(1)}, u32[]{:S(2)}, u32[]{:S(2)}) collective-permute-start(bf16[2,128,128]{2,1,0:T(8,128)(2,1)S(1)} %fusion.176), channel_id=1, source_target_pairs={{0,16},{16,32},{32,48},{48,64},{64,80},{80,96},{96,112},{112,128},... | collective-permute-start | bytes 196616 | tf_op jit(solution)/shard_map/while/body/eval_jaxpr/ppermute | solution.py:12
  336.8 5.9 %collective-permute-start = (bf16[2,128,128]{2,1,0:T(8,128)(2,1)S(1)}, bf16[2,128,128]{2,1,0:T(8,128)(2,1)S(1)}, u32[]{:S(2)}, u32[]{:S(2)}) collective-permute-start(bf16[2,128,128]{2,1,0:T(8,128)(2,1)S(1)} %fusion.176), channel_id=1, source_target_pairs={{0,16},{16,32},{32,48},{48,64},{64,80},{80,96},{96,112},{112,128},... | collective-permute-start | bytes 196616 | tf_op jit(solution)/shard_map/while/body/eval_jaxpr/ppermute | solution.py:12
  343.9 5.9 %collective-permute-start = (bf16[2,128,128]{2,1,0:T(8,128)(2,1)S(1)}, bf16[2,128,128]{2,1,0:T(8,128)(2,1)S(1)}, u32[]{:S(2)}, u32[]{:S(2)}) collective-permute-start(bf16[2,128,128]{2,1,0:T(8,128)(2,1)S(1)} %fusion.176), channel_id=1, source_target_pairs={{0,16},{16,32},{32,48},{48,64},{64,80},{80,96},{96,112},{112,128},... | collective-permute-start | bytes 196616 | tf_op jit(solution)/shard_map/while/body/eval_jaxpr/ppermute | solution.py:12
  351.0 5.9 %collective-permute-start = (bf16[2,128,128]{2,1,0:T(8,128)(2,1)S(1)}, bf16[2,128,128]{2,1,0:T(8,128)(2,1)S(1)}, u32[]{:S(2)}, u32[]{:S(2)}) collective-permute-start(bf16[2,128,128]{2,1,0:T(8,128)(2,1)S(1)} %fusion.176), channel_id=1, source_target_pairs={{0,16},{16,32},{32,48},{48,64},{64,80},{80,96},{96,112},{112,128},... | collective-permute-start | bytes 196616 | tf_op jit(solution)/shard_map/while/body/eval_jaxpr/ppermute | solution.py:12
  357.8 52.2 %while.36 = (s32[]{:T(128)}, f32[2,128,128]{2,1,0:T(8,128)S(1)}, f32[2,2,128,128]{3,2,1,0:T(8,128)}, s32[2,128]{1,0:T(2,128)S(1)}, f32[2,2,128,128]{3,2,1,0:T(8,...) while((s32[]{:T(128)}, f32[2,128,128]{2,1,0:T(8,128)S(1)}, ...), condition=%wide.region_9.11_spmd, body=%wide.region_8.10_spmd.sunk | while | flops 504103552 | bytes 7187665 | solution.py:121
  358.4 19.7 %custom-call.11 = f32[2,1,128,128]{2,3,1,0:T(8,128)S(1)} custom-call(f32[2,1,128,128]{3,2,1,0:T(8,128)S(1)} %fusion.154), custom_call_target="InvertDiagBlocksLowerTriangular" | custom-call | tf_op jit(solution)/shard_map/while/body/eval_jaxpr/jit(_solve_triangular)/vmap()/triangular_solve | solution.py:41
  384.5 19.7 %custom-call.11 = f32[2,1,128,128]{2,3,1,0:T(8,128)S(1)} custom-call(f32[2,1,128,128]{3,2,1,0:T(8,128)S(1)} %fusion.154), custom_call_target="InvertDiagBlocksLowerTriangular" | custom-call | tf_op jit(solution)/shard_map/while/body/eval_jaxpr/jit(_solve_triangular)/vmap()/triangular_solve | solution.py:41
  416.5 111.2 %reduce-scatter.2.cloned.1.call-done = bf16[256,256]{1,0:T(8,128)(2,1)} async-done(((bf16[256,4096]{1,0:T(8,128)(2,1)}), bf16[256,256]{1,0:T(8,128)(2,1)}) %reduce-scatter.2.cloned.1.call-update) | async-done | bytes 131088 | tf_op jit(solution)/shard_map/reduce_scatter | solution.py:128
  (227 shorter events, 113.9 us)
Async XLA Ops:
  6.5 95.9 %all-gather.3.cloned.1.call-start = ((), (), s32[]{:S(2)}) async-start(), calls=%async_computation.1 | async-start | bytes 6488064 | tf_op jit(solution)/shard_map/all_gather | solution.py:67
  8.5 404.0 %all-gather.5.cloned.1.call-start = ((), (), s32[]{:S(2)}) async-start(), calls=%async_computation.2 | async-start | bytes 2162688 | tf_op jit(solution)/shard_map/all_gather | solution.py:126
  9.2 518.5 %reduce-scatter.2.cloned.1.call-start = ((), (), s32[]{:S(2)}) async-start(), calls=%async_computation.3 | async-start | bytes 2228224 | tf_op jit(solution)/shard_map/reduce_scatter | solution.py:128
  171.3 5.6 %collective-permute-start = (bf16[2,128,128]{2,1,0:T(8,128)(2,1)S(1)}, bf16[2,128,128]{2,1,0:T(8,128)(2,1)S(1)}, u32[]{:S(2)}, u32[]{:S(2)}) collective-permute-start(bf16[2,128,128]{2,1,0:T(8,128)(2,1)S(1)} %fusion.176), channel_id=1, source_target_pairs={{0,16},{16,32},{32,48},{48,64},{64,80},{80,96},{96,112},{112,128},... | collective-permute-start | bytes 196616 | tf_op jit(solution)/shard_map/while/body/eval_jaxpr/ppermute | solution.py:12
  177.2 5.6 %collective-permute-start = (bf16[2,128,128]{2,1,0:T(8,128)(2,1)S(1)}, bf16[2,128,128]{2,1,0:T(8,128)(2,1)S(1)}, u32[]{:S(2)}, u32[]{:S(2)}) collective-permute-start(bf16[2,128,128]{2,1,0:T(8,128)(2,1)S(1)} %fusion.176), channel_id=1, source_target_pairs={{0,16},{16,32},{32,48},{48,64},{64,80},{80,96},{96,112},{112,128},... | collective-permute-start | bytes 196616 | tf_op jit(solution)/shard_map/while/body/eval_jaxpr/ppermute | solution.py:12
  183.1 5.6 %collective-permute-start = (bf16[2,128,128]{2,1,0:T(8,128)(2,1)S(1)}, bf16[2,128,128]{2,1,0:T(8,128)(2,1)S(1)}, u32[]{:S(2)}, u32[]{:S(2)}) collective-permute-start(bf16[2,128,128]{2,1,0:T(8,128)(2,1)S(1)} %fusion.176), channel_id=1, source_target_pairs={{0,16},{16,32},{32,48},{48,64},{64,80},{80,96},{96,112},{112,128},... | collective-permute-start | bytes 196616 | tf_op jit(solution)/shard_map/while/body/eval_jaxpr/ppermute | solution.py:12
  189.0 5.6 %collective-permute-start = (bf16[2,128,128]{2,1,0:T(8,128)(2,1)S(1)}, bf16[2,128,128]{2,1,0:T(8,128)(2,1)S(1)}, u32[]{:S(2)}, u32[]{:S(2)}) collective-permute-start(bf16[2,128,128]{2,1,0:T(8,128)(2,1)S(1)} %fusion.176), channel_id=1, source_target_pairs={{0,16},{16,32},{32,48},{48,64},{64,80},{80,96},{96,112},{112,128},... | collective-permute-start | bytes 196616 | tf_op jit(solution)/shard_map/while/body/eval_jaxpr/ppermute | solution.py:12
  194.9 5.6 %collective-permute-start = (bf16[2,128,128]{2,1,0:T(8,128)(2,1)S(1)}, bf16[2,128,128]{2,1,0:T(8,128)(2,1)S(1)}, u32[]{:S(2)}, u32[]{:S(2)}) collective-permute-start(bf16[2,128,128]{2,1,0:T(8,128)(2,1)S(1)} %fusion.176), channel_id=1, source_target_pairs={{0,16},{16,32},{32,48},{48,64},{64,80},{80,96},{96,112},{112,128},... | collective-permute-start | bytes 196616 | tf_op jit(solution)/shard_map/while/body/eval_jaxpr/ppermute | solution.py:12
  200.8 5.6 %collective-permute-start = (bf16[2,128,128]{2,1,0:T(8,128)(2,1)S(1)}, bf16[2,128,128]{2,1,0:T(8,128)(2,1)S(1)}, u32[]{:S(2)}, u32[]{:S(2)}) collective-permute-start(bf16[2,128,128]{2,1,0:T(8,128)(2,1)S(1)} %fusion.176), channel_id=1, source_target_pairs={{0,16},{16,32},{32,48},{48,64},{64,80},{80,96},{96,112},{112,128},... | collective-permute-start | bytes 196616 | tf_op jit(solution)/shard_map/while/body/eval_jaxpr/ppermute | solution.py:12
  206.7 5.6 %collective-permute-start = (bf16[2,128,128]{2,1,0:T(8,128)(2,1)S(1)}, bf16[2,128,128]{2,1,0:T(8,128)(2,1)S(1)}, u32[]{:S(2)}, u32[]{:S(2)}) collective-permute-start(bf16[2,128,128]{2,1,0:T(8,128)(2,1)S(1)} %fusion.176), channel_id=1, source_target_pairs={{0,16},{16,32},{32,48},{48,64},{64,80},{80,96},{96,112},{112,128},... | collective-permute-start | bytes 196616 | tf_op jit(solution)/shard_map/while/body/eval_jaxpr/ppermute | solution.py:12
  212.6 5.6 %collective-permute-start = (bf16[2,128,128]{2,1,0:T(8,128)(2,1)S(1)}, bf16[2,128,128]{2,1,0:T(8,128)(2,1)S(1)}, u32[]{:S(2)}, u32[]{:S(2)}) collective-permute-start(bf16[2,128,128]{2,1,0:T(8,128)(2,1)S(1)} %fusion.176), channel_id=1, source_target_pairs={{0,16},{16,32},{32,48},{48,64},{64,80},{80,96},{96,112},{112,128},... | collective-permute-start | bytes 196616 | tf_op jit(solution)/shard_map/while/body/eval_jaxpr/ppermute | solution.py:12
  218.5 5.6 %collective-permute-start = (bf16[2,128,128]{2,1,0:T(8,128)(2,1)S(1)}, bf16[2,128,128]{2,1,0:T(8,128)(2,1)S(1)}, u32[]{:S(2)}, u32[]{:S(2)}) collective-permute-start(bf16[2,128,128]{2,1,0:T(8,128)(2,1)S(1)} %fusion.176), channel_id=1, source_target_pairs={{0,16},{16,32},{32,48},{48,64},{64,80},{80,96},{96,112},{112,128},... | collective-permute-start | bytes 196616 | tf_op jit(solution)/shard_map/while/body/eval_jaxpr/ppermute | solution.py:12
  224.4 5.6 %collective-permute-start = (bf16[2,128,128]{2,1,0:T(8,128)(2,1)S(1)}, bf16[2,128,128]{2,1,0:T(8,128)(2,1)S(1)}, u32[]{:S(2)}, u32[]{:S(2)}) collective-permute-start(bf16[2,128,128]{2,1,0:T(8,128)(2,1)S(1)} %fusion.176), channel_id=1, source_target_pairs={{0,16},{16,32},{32,48},{48,64},{64,80},{80,96},{96,112},{112,128},... | collective-permute-start | bytes 196616 | tf_op jit(solution)/shard_map/while/body/eval_jaxpr/ppermute | solution.py:12
  230.3 5.6 %collective-permute-start = (bf16[2,128,128]{2,1,0:T(8,128)(2,1)S(1)}, bf16[2,128,128]{2,1,0:T(8,128)(2,1)S(1)}, u32[]{:S(2)}, u32[]{:S(2)}) collective-permute-start(bf16[2,128,128]{2,1,0:T(8,128)(2,1)S(1)} %fusion.176), channel_id=1, source_target_pairs={{0,16},{16,32},{32,48},{48,64},{64,80},{80,96},{96,112},{112,128},... | collective-permute-start | bytes 196616 | tf_op jit(solution)/shard_map/while/body/eval_jaxpr/ppermute | solution.py:12
  236.2 5.6 %collective-permute-start = (bf16[2,128,128]{2,1,0:T(8,128)(2,1)S(1)}, bf16[2,128,128]{2,1,0:T(8,128)(2,1)S(1)}, u32[]{:S(2)}, u32[]{:S(2)}) collective-permute-start(bf16[2,128,128]{2,1,0:T(8,128)(2,1)S(1)} %fusion.176), channel_id=1, source_target_pairs={{0,16},{16,32},{32,48},{48,64},{64,80},{80,96},{96,112},{112,128},... | collective-permute-start | bytes 196616 | tf_op jit(solution)/shard_map/while/body/eval_jaxpr/ppermute | solution.py:12
  242.0 5.6 %collective-permute-start = (bf16[2,128,128]{2,1,0:T(8,128)(2,1)S(1)}, bf16[2,128,128]{2,1,0:T(8,128)(2,1)S(1)}, u32[]{:S(2)}, u32[]{:S(2)}) collective-permute-start(bf16[2,128,128]{2,1,0:T(8,128)(2,1)S(1)} %fusion.176), channel_id=1, source_target_pairs={{0,16},{16,32},{32,48},{48,64},{64,80},{80,96},{96,112},{112,128},... | collective-permute-start | bytes 196616 | tf_op jit(solution)/shard_map/while/body/eval_jaxpr/ppermute | solution.py:12
  247.9 5.6 %collective-permute-start = (bf16[2,128,128]{2,1,0:T(8,128)(2,1)S(1)}, bf16[2,128,128]{2,1,0:T(8,128)(2,1)S(1)}, u32[]{:S(2)}, u32[]{:S(2)}) collective-permute-start(bf16[2,128,128]{2,1,0:T(8,128)(2,1)S(1)} %fusion.176), channel_id=1, source_target_pairs={{0,16},{16,32},{32,48},{48,64},{64,80},{80,96},{96,112},{112,128},... | collective-permute-start | bytes 196616 | tf_op jit(solution)/shard_map/while/body/eval_jaxpr/ppermute | solution.py:12
  253.8 5.6 %collective-permute-start = (bf16[2,128,128]{2,1,0:T(8,128)(2,1)S(1)}, bf16[2,128,128]{2,1,0:T(8,128)(2,1)S(1)}, u32[]{:S(2)}, u32[]{:S(2)}) collective-permute-start(bf16[2,128,128]{2,1,0:T(8,128)(2,1)S(1)} %fusion.176), channel_id=1, source_target_pairs={{0,16},{16,32},{32,48},{48,64},{64,80},{80,96},{96,112},{112,128},... | collective-permute-start | bytes 196616 | tf_op jit(solution)/shard_map/while/body/eval_jaxpr/ppermute | solution.py:12
  259.7 5.7 %collective-permute-start = (bf16[2,128,128]{2,1,0:T(8,128)(2,1)S(1)}, bf16[2,128,128]{2,1,0:T(8,128)(2,1)S(1)}, u32[]{:S(2)}, u32[]{:S(2)}) collective-permute-start(bf16[2,128,128]{2,1,0:T(8,128)(2,1)S(1)} %fusion.176), channel_id=1, source_target_pairs={{0,16},{16,32},{32,48},{48,64},{64,80},{80,96},{96,112},{112,128},... | collective-permute-start | bytes 196616 | tf_op jit(solution)/shard_map/while/body/eval_jaxpr/ppermute | solution.py:12
  265.7 6.8 %collective-permute-start = (bf16[2,128,128]{2,1,0:T(8,128)(2,1)S(1)}, bf16[2,128,128]{2,1,0:T(8,128)(2,1)S(1)}, u32[]{:S(2)}, u32[]{:S(2)}) collective-permute-start(bf16[2,128,128]{2,1,0:T(8,128)(2,1)S(1)} %fusion.176), channel_id=1, source_target_pairs={{0,16},{16,32},{32,48},{48,64},{64,80},{80,96},{96,112},{112,128},... | collective-permute-start | bytes 196616 | tf_op jit(solution)/shard_map/while/body/eval_jaxpr/ppermute | solution.py:12
  272.8 6.8 %collective-permute-start = (bf16[2,128,128]{2,1,0:T(8,128)(2,1)S(1)}, bf16[2,128,128]{2,1,0:T(8,128)(2,1)S(1)}, u32[]{:S(2)}, u32[]{:S(2)}) collective-permute-start(bf16[2,128,128]{2,1,0:T(8,128)(2,1)S(1)} %fusion.176), channel_id=1, source_target_pairs={{0,16},{16,32},{32,48},{48,64},{64,80},{80,96},{96,112},{112,128},... | collective-permute-start | bytes 196616 | tf_op jit(solution)/shard_map/while/body/eval_jaxpr/ppermute | solution.py:12
  279.9 6.8 %collective-permute-start = (bf16[2,128,128]{2,1,0:T(8,128)(2,1)S(1)}, bf16[2,128,128]{2,1,0:T(8,128)(2,1)S(1)}, u32[]{:S(2)}, u32[]{:S(2)}) collective-permute-start(bf16[2,128,128]{2,1,0:T(8,128)(2,1)S(1)} %fusion.176), channel_id=1, source_target_pairs={{0,16},{16,32},{32,48},{48,64},{64,80},{80,96},{96,112},{112,128},... | collective-permute-start | bytes 196616 | tf_op jit(solution)/shard_map/while/body/eval_jaxpr/ppermute | solution.py:12
  287.0 6.8 %collective-permute-start = (bf16[2,128,128]{2,1,0:T(8,128)(2,1)S(1)}, bf16[2,128,128]{2,1,0:T(8,128)(2,1)S(1)}, u32[]{:S(2)}, u32[]{:S(2)}) collective-permute-start(bf16[2,128,128]{2,1,0:T(8,128)(2,1)S(1)} %fusion.176), channel_id=1, source_target_pairs={{0,16},{16,32},{32,48},{48,64},{64,80},{80,96},{96,112},{112,128},... | collective-permute-start | bytes 196616 | tf_op jit(solution)/shard_map/while/body/eval_jaxpr/ppermute | solution.py:12
  294.2 6.8 %collective-permute-start = (bf16[2,128,128]{2,1,0:T(8,128)(2,1)S(1)}, bf16[2,128,128]{2,1,0:T(8,128)(2,1)S(1)}, u32[]{:S(2)}, u32[]{:S(2)}) collective-permute-start(bf16[2,128,128]{2,1,0:T(8,128)(2,1)S(1)} %fusion.176), channel_id=1, source_target_pairs={{0,16},{16,32},{32,48},{48,64},{64,80},{80,96},{96,112},{112,128},... | collective-permute-start | bytes 196616 | tf_op jit(solution)/shard_map/while/body/eval_jaxpr/ppermute | solution.py:12
  301.3 6.8 %collective-permute-start = (bf16[2,128,128]{2,1,0:T(8,128)(2,1)S(1)}, bf16[2,128,128]{2,1,0:T(8,128)(2,1)S(1)}, u32[]{:S(2)}, u32[]{:S(2)}) collective-permute-start(bf16[2,128,128]{2,1,0:T(8,128)(2,1)S(1)} %fusion.176), channel_id=1, source_target_pairs={{0,16},{16,32},{32,48},{48,64},{64,80},{80,96},{96,112},{112,128},... | collective-permute-start | bytes 196616 | tf_op jit(solution)/shard_map/while/body/eval_jaxpr/ppermute | solution.py:12
  308.4 6.8 %collective-permute-start = (bf16[2,128,128]{2,1,0:T(8,128)(2,1)S(1)}, bf16[2,128,128]{2,1,0:T(8,128)(2,1)S(1)}, u32[]{:S(2)}, u32[]{:S(2)}) collective-permute-start(bf16[2,128,128]{2,1,0:T(8,128)(2,1)S(1)} %fusion.176), channel_id=1, source_target_pairs={{0,16},{16,32},{32,48},{48,64},{64,80},{80,96},{96,112},{112,128},... | collective-permute-start | bytes 196616 | tf_op jit(solution)/shard_map/while/body/eval_jaxpr/ppermute | solution.py:12
  315.5 6.8 %collective-permute-start = (bf16[2,128,128]{2,1,0:T(8,128)(2,1)S(1)}, bf16[2,128,128]{2,1,0:T(8,128)(2,1)S(1)}, u32[]{:S(2)}, u32[]{:S(2)}) collective-permute-start(bf16[2,128,128]{2,1,0:T(8,128)(2,1)S(1)} %fusion.176), channel_id=1, source_target_pairs={{0,16},{16,32},{32,48},{48,64},{64,80},{80,96},{96,112},{112,128},... | collective-permute-start | bytes 196616 | tf_op jit(solution)/shard_map/while/body/eval_jaxpr/ppermute | solution.py:12
  322.6 6.8 %collective-permute-start = (bf16[2,128,128]{2,1,0:T(8,128)(2,1)S(1)}, bf16[2,128,128]{2,1,0:T(8,128)(2,1)S(1)}, u32[]{:S(2)}, u32[]{:S(2)}) collective-permute-start(bf16[2,128,128]{2,1,0:T(8,128)(2,1)S(1)} %fusion.176), channel_id=1, source_target_pairs={{0,16},{16,32},{32,48},{48,64},{64,80},{80,96},{96,112},{112,128},... | collective-permute-start | bytes 196616 | tf_op jit(solution)/shard_map/while/body/eval_jaxpr/ppermute | solution.py:12
  329.7 6.8 %collective-permute-start = (bf16[2,128,128]{2,1,0:T(8,128)(2,1)S(1)}, bf16[2,128,128]{2,1,0:T(8,128)(2,1)S(1)}, u32[]{:S(2)}, u32[]{:S(2)}) collective-permute-start(bf16[2,128,128]{2,1,0:T(8,128)(2,1)S(1)} %fusion.176), channel_id=1, source_target_pairs={{0,16},{16,32},{32,48},{48,64},{64,80},{80,96},{96,112},{112,128},... | collective-permute-start | bytes 196616 | tf_op jit(solution)/shard_map/while/body/eval_jaxpr/ppermute | solution.py:12
  336.8 6.8 %collective-permute-start = (bf16[2,128,128]{2,1,0:T(8,128)(2,1)S(1)}, bf16[2,128,128]{2,1,0:T(8,128)(2,1)S(1)}, u32[]{:S(2)}, u32[]{:S(2)}) collective-permute-start(bf16[2,128,128]{2,1,0:T(8,128)(2,1)S(1)} %fusion.176), channel_id=1, source_target_pairs={{0,16},{16,32},{32,48},{48,64},{64,80},{80,96},{96,112},{112,128},... | collective-permute-start | bytes 196616 | tf_op jit(solution)/shard_map/while/body/eval_jaxpr/ppermute | solution.py:12
  343.9 6.8 %collective-permute-start = (bf16[2,128,128]{2,1,0:T(8,128)(2,1)S(1)}, bf16[2,128,128]{2,1,0:T(8,128)(2,1)S(1)}, u32[]{:S(2)}, u32[]{:S(2)}) collective-permute-start(bf16[2,128,128]{2,1,0:T(8,128)(2,1)S(1)} %fusion.176), channel_id=1, source_target_pairs={{0,16},{16,32},{32,48},{48,64},{64,80},{80,96},{96,112},{112,128},... | collective-permute-start | bytes 196616 | tf_op jit(solution)/shard_map/while/body/eval_jaxpr/ppermute | solution.py:12
  351.0 6.8 %collective-permute-start = (bf16[2,128,128]{2,1,0:T(8,128)(2,1)S(1)}, bf16[2,128,128]{2,1,0:T(8,128)(2,1)S(1)}, u32[]{:S(2)}, u32[]{:S(2)}) collective-permute-start(bf16[2,128,128]{2,1,0:T(8,128)(2,1)S(1)} %fusion.176), channel_id=1, source_target_pairs={{0,16},{16,32},{32,48},{48,64},{64,80},{80,96},{96,112},{112,128},... | collective-permute-start | bytes 196616 | tf_op jit(solution)/shard_map/while/body/eval_jaxpr/ppermute | solution.py:12
  (8 other events, 307.5 us)
Sparse Core Ops, SparseCore 0:
  9.4 92.9 all-gather.2
  104.5 69.6 all-gather.4
  416.6 111.0 reduce-scatter.1
where the time goes:
time: 535 us; the launch traced here: 534 us
  waiting for transfers between devices  231 us (43%)
  starting transfers between devices  157 us (29%)
  other arithmetic  90.8 us (17%)
  matrix products  27.9 us (5%)
  between operations  13.3 us (2%)
  local copies, waits for them, and re-layouts  12.8 us (2%)
    ppermute x31, starting transfers between devices, passed_along(): lax.ppermute(value, axis, [(source, source + steps) for source in range(f...  157 us
    reduce_scatter x1, waiting for transfers between devices, per_device(): lax.psum_scatter(terms.astype(jnp.bfloat16), 'head', scatter_dimension=1,...  111 us
    all_gather x1, waiting for transfers between devices, per_device(): lax.all_gather(w_qkv, 'seq', axis=1, tiled=True)  91.4 us
    another operation x10, other arithmetic, block_terms(): jax.scipy.linalg.solve_triangular(system, right_side, lower=True, unit_di...  78.9 us
    ppermute x31, waiting for transfers between devices, passed_along(): lax.ppermute(value, axis, [(source, source + steps) for source in range(f...  27.3 us
    dot_general x43, matrix products, bmatmul(): return jnp.einsum('hij,hjk->hik', left, right, precision=highest_accuracy)  11.6 us
  transfers between devices with their start and end apart: 34, of which 33 were waited for; matrix products, arithmetic and copies ran while one was open for 24% of the time, Pallas kernels for 0%

commit v1 on v0

--- a/solution.py
+++ b/solution.py
@@ -4,6 +4,11 @@
 from jax.sharding import PartitionSpec as P
 
 highest_accuracy = lax.Precision.HIGHEST
+
+
+def all_by_exchange(x, axis, d):
+    outgoing = jnp.stack([x] * lax.axis_size(axis))
+    return jnp.concatenate(lax.all_to_all(outgoing, axis, 0, 0), axis=d)
 
 
 def passed_along(value, axis, steps):
@@ -64,7 +69,7 @@
     projected = jnp.einsum(
         "td,pde->pte",
         hidden_in,
-        lax.all_gather(w_qkv, "seq", axis=1, tiled=True),
+        all_by_exchange(w_qkv, "seq", 1),
         preferred_element_type=jnp.float32,
     ).astype(jnp.bfloat16)
     block_len = min(128, tok_rows)

time: 535 us -> 750 us (1.40)
  the two profiles are of different devices: /device:TPU:2 before, /device:TPU:32 now
where the time goes in v1:
time: 750 us; the launch traced here: 749 us
  waiting for transfers between devices  475 us (63%)
  starting transfers between devices  121 us (16%)
  other arithmetic  92.7 us (12%)
  matrix products  27.9 us (4%)
  local copies, waits for them, and re-layouts  16.4 us (2%)
  between operations  13.6 us (2%)
    all_to_all x1, waiting for transfers between devices, all_by_exchange(): return jnp.concatenate(lax.all_to_all(outgoing, axis, 0, 0), axis=d)  289 us
    reduce_scatter x1, waiting for transfers between devices, per_device(): lax.psum_scatter(terms.astype(jnp.bfloat16), 'head', scatter_dimension=1,...  106 us
    ppermute x31, starting transfers between devices, passed_along(): lax.ppermute(value, axis, [(source, source + steps) for source in range(f...  106 us
    ppermute x31, waiting for transfers between devices, passed_along(): lax.ppermute(value, axis, [(source, source + steps) for source in range(f...  79.8 us
    another operation x10, other arithmetic, block_terms(): jax.scipy.linalg.solve_triangular(system, right_side, lower=True, unit_di...  78.9 us
    all_to_all x1, starting transfers between devices, all_by_exchange(): return jnp.concatenate(lax.all_to_all(outgoing, axis, 0, 0), axis=d)  15.5 us
  transfers between devices with their start and end apart: 34, of which 33 were waited for; matrix products, arithmetic and copies ran while one was open for 17% of the time, Pallas kernels for 0%

profile of v1, /device:TPU:32, one launch (start us, length us, event | category | flops | bytes accessed | tf_op | source)
XLA Modules:
  0.0 749.1 jit_solution(806952055239590490)
XLA Ops:
  7.8 4.2 stack.2
  12.0 15.5 %all-to-all-start = ((bf16[32,3,128,256]{2,3,1,0:T(8,128)(2,1)}), bf16[32,3,128,256]{2,3,1,0:T(8,128)(2,1)}, u32[]{:S(2)}, u32[]{:S(2)}) async-start(bf16[32,3,128,256]{2,3,1,0:T(8,128)(2,1)} %stack.2), calls=%async_computation | async-start | bytes 12582912 | tf_op jit(solution)/shard_map/all_to_all | solution.py:11
  29.4 288.8 %all-to-all-done = bf16[32,3,128,256]{2,3,1,0:T(8,128)(2,1)} async-done(((bf16[32,3,128,256]{2,3,1,0:T(8,128)(2,1)}), bf16[32,3,128,256]{2,3,1,0:T(8,128)(2,1)}, u32[]{:S(2)}, u32[]{:S(2)}) %all-to-all-start) | async-done | bytes 6291488 | tf_op jit(solution)/shard_map/all_to_all | solution.py:11
  318.1 4.6 fusion.81
  329.8 51.5 %while.37 = (s32[]{:T(128)}, f32[2,128,128]{2,1,0:T(8,128)S(1)}, f32[2,128,128]{2,1,0:T(8,128)S(1)}, s32[2,128]{1,0:T(2,128)}, f32[2,2,128,128]{3,2,1,0:T(8,128)...) while((s32[]{:T(128)}, f32[2,128,128]{2,1,0:T(8,128)S(1)}, ...), condition=%wide.region_4.6_spmd.clone, body=%wide.region_3.5_spmd.clone.sunk | while | flops 352977536 | bytes 3876507 | solution.py:110
  331.3 19.7 %custom-call.12 = f32[2,1,128,128]{2,3,1,0:T(8,128)S(1)} custom-call(f32[2,1,128,128]{3,2,1,0:T(8,128)S(1)} %fusion.175), custom_call_target="InvertDiagBlocksLowerTriangular" | custom-call | tf_op jit(solution)/shard_map/while/body/eval_jaxpr/jit(_solve_triangular)/vmap()/triangular_solve | solution.py:46
  357.0 19.7 %custom-call.12 = f32[2,1,128,128]{2,3,1,0:T(8,128)S(1)} custom-call(f32[2,1,128,128]{3,2,1,0:T(8,128)S(1)} %fusion.175), custom_call_target="InvertDiagBlocksLowerTriangular" | custom-call | tf_op jit(solution)/shard_map/while/body/eval_jaxpr/jit(_solve_triangular)/vmap()/triangular_solve | solution.py:46
  381.3 195.4 %while.38 = (s32[]{:T(128)}, f32[2,128,128]{2,1,0:T(8,128)S(1)}, f32[2,128,128]{2,1,0:T(8,128)S(1)}, f32[2,128,128]{2,1,0:T(8,128)S(1)}, s32[]{:T(128)}, /*index=5*/s32[]{:T(128)}) while((s32[]{:T(128)}, f32[2,128,128]{2,1,0:T(8,128)S(1)}, f32[2,128,128]{2,1,0:T(8,128)S(1)}, f32[2,128,128]{2,1,0:T(8,128)S(1)}, s32[]{:T(128)}, ...), condition=%wide.region_6.8_spmd.clone, body=%wide.region_5.7_spmd.clone.sunk | while | flops 50462720 | bytes 917623 | solution.py:119
  383.6 3.7 collective-permute-done
  389.5 3.7 collective-permute-done
  395.4 3.7 collective-permute-done
  401.3 3.7 collective-permute-done
  407.1 3.7 collective-permute-done
  413.0 3.7 collective-permute-done
  418.9 3.7 collective-permute-done
  493.6 4.0 collective-permute-start
  499.5 5.2 collective-permute-start
  506.0 5.9 collective-permute-start
  513.1 5.9 collective-permute-start
  520.2 5.9 collective-permute-start
  527.3 5.9 collective-permute-start
  534.4 5.9 collective-permute-start
  541.5 5.9 collective-permute-start
  548.6 5.9 collective-permute-start
  555.7 5.9 collective-permute-start
  562.8 5.9 collective-permute-start
  569.9 5.9 collective-permute-start
  576.7 53.2 %while.36 = (s32[]{:T(128)}, f32[2,128,128]{2,1,0:T(8,128)S(1)}, f32[2,2,128,128]{3,2,1,0:T(8,128)}, s32[2,128]{1,0:T(2,128)}, f32[2,2,128,128]{3,2,1,0:T(8,128)...) while((s32[]{:T(128)}, f32[2,128,128]{2,1,0:T(8,128)S(1)}, ...), condition=%wide.region_9.11_spmd, body=%wide.region_8.10_spmd.sunk | while | flops 504103552 | bytes 7187665 | solution.py:126
  578.0 19.7 %custom-call.11 = f32[2,1,128,128]{2,3,1,0:T(8,128)S(1)} custom-call(f32[2,1,128,128]{3,2,1,0:T(8,128)S(1)} %fusion.160), custom_call_target="InvertDiagBlocksLowerTriangular" | custom-call | tf_op jit(solution)/shard_map/while/body/eval_jaxpr/jit(_solve_triangular)/vmap()/triangular_solve | solution.py:46
  604.6 19.7 %custom-call.11 = f32[2,1,128,128]{2,3,1,0:T(8,128)S(1)} custom-call(f32[2,1,128,128]{3,2,1,0:T(8,128)S(1)} %fusion.160), custom_call_target="InvertDiagBlocksLowerTriangular" | custom-call | tf_op jit(solution)/shard_map/while/body/eval_jaxpr/jit(_solve_triangular)/vmap()/triangular_solve | solution.py:46
  632.7 3.7 convolution_convert_fusion
  636.4 105.9 %reduce-scatter.2.cloned.1.call-done = bf16[256,256]{1,0:T(8,128)(2,1)} async-done(((bf16[256,4096]{1,0:T(8,128)(2,1)}), bf16[256,256]{1,0:T(8,128)(2,1)}) %reduce-scatter.2.cloned.1.call-update) | async-done | bytes 131088 | tf_op jit(solution)/shard_map/reduce_scatter | solution.py:133
  (231 shorter events, 138.3 us)
Async XLA Ops:
  12.0 306.2 %all-to-all-start = ((bf16[32,3,128,256]{2,3,1,0:T(8,128)(2,1)}), bf16[32,3,128,256]{2,3,1,0:T(8,128)(2,1)}, u32[]{:S(2)}, u32[]{:S(2)}) async-start(bf16[32,3,128,256]{2,3,1,0:T(8,128)(2,1)} %stack.2), calls=%async_computation | async-start | bytes 12582912 | tf_op jit(solution)/shard_map/all_to_all | solution.py:11
  27.5 604.9 %all-gather.2.cloned.1.call-start = ((), (), s32[]{:S(2)}) async-start(), calls=%async_computation.2 | async-start | bytes 2162688 | tf_op jit(solution)/shard_map/all_gather | solution.py:131
  28.3 714.0 %reduce-scatter.2.cloned.1.call-start = ((), (), s32[]{:S(2)}) async-start(), calls=%async_computation.3 | async-start | bytes 2228224 | tf_op jit(solution)/shard_map/reduce_scatter | solution.py:133
  381.6 5.6 collective-permute-start
  387.5 5.6 collective-permute-start
  393.4 5.6 collective-permute-start
  399.3 5.6 collective-permute-start
  405.2 5.6 collective-permute-start
  411.1 5.6 collective-permute-start
  417.0 5.6 collective-permute-start
  422.9 5.6 collective-permute-start
  428.8 5.6 collective-permute-start
  434.7 5.6 collective-permute-start
  446.5 5.6 collective-permute-start
  452.4 5.6 collective-permute-start
  458.3 5.6 collective-permute-start
  464.2 5.6 collective-permute-start
  470.1 5.6 collective-permute-start
  481.8 5.6 collective-permute-start
  487.7 5.6 collective-permute-start
  493.6 5.6 collective-permute-start
  499.5 6.1 collective-permute-start
  506.0 6.8 collective-permute-start
  513.1 6.8 collective-permute-start
  520.2 6.8 collective-permute-start
  527.3 6.8 collective-permute-start
  534.4 6.8 collective-permute-start
  541.5 6.8 collective-permute-start
  548.6 6.8 collective-permute-start
  555.7 6.8 collective-permute-start
  562.8 6.8 collective-permute-start
  569.9 6.8 collective-permute-start
  (10 other events, 562.6 us)
Sparse Core Ops, SparseCore 0:
  30.4 152.9 all-gather.1
  636.5 105.6 reduce-scatter.1
